TPU v7x, 32 devices: a whole 2x2x4 slice. The times are simulated.
32 devices in a mesh: copy: 2 (over y), grid: 4 (over z), blk: 2 (over x), sub: 2 (over core).
Axes of the slice: x: 2, y: 2, z: 4, core: 2. Of those that a mesh axis runs over, the one named last changes fastest.
Arguments:
- ensemble: float32 [128, 3, 256, 1024], P(('copy', 'grid'), None, 'blk', 'sub'), parts along dimension 0, may hold values from -6 to 6
- basin_thickness: float32 [512, 1024], P(('copy', 'blk'), 'sub'), parts along dimension 0, may hold values from 0.25 to 2
- wet_indicator: int32 [512, 1024], P(('copy', 'blk'), 'sub'), parts along dimension 0, may hold values 0 or 1
- obs_cell: int32 [4, 4, 2, 64], P(('copy', 'blk'), 'grid', 'sub'), parts along dimension 0, may hold values from 0 to 16383
- obs_count: int32 [4, 4, 2], P(('copy', 'blk'), 'grid', 'sub'), parts along dimension 0, may hold values from 16 to 64, as said below
- obs_value: float32 [4, 4, 2, 64], P(('copy', 'blk'), 'grid', 'sub'), parts along dimension 0, may hold values from -6 to 6
- obs_error: float32 [4, 4, 2, 64], P(('copy', 'blk'), 'grid', 'sub'), parts along dimension 0, may hold values from 0.5 to 2
Outputs:
- analysis: float32 [128, 3, 2, 128, 1024], P('copy', None, 'blk', 'grid', 'sub'), parts along dimension 0
There are 2 independent parts, one for each index of `copy`. A program takes and returns all parts, laid end to end along the dimension named above; each array names one. Nothing has to cross between parts.
Inputs may be any that keep to these rules, and one draw needn't show every extreme that they name: `obs_count`: one block of every draw has all 64 slots live.
All inputs are finite; a program needn't handle non-finite values. No bound on the sum of `wet_indicator` on one device may be relied on, other than what follows from the above.
Results may differ from a plain program's by a relative error of at most 0.0003.
Values sent between devices are 32-bit elements; how exact they have to be, the bound alone decides.
No kernel may reach another device: no remote copies, remote signals or barrier semaphores. Data moves between devices by JAX's collectives and lax.ppermute only.
A program may use at most 128 MiB of HBM per device.

v0:
```python
import math

import jax
import jax.numpy as jnp
from jax import lax
from jax.sharding import PartitionSpec as P

STEPS = 2
NS_STEPS = 8


FRICTION = 0.05
PRESSURE = 0.35
DIVERGE = 0.35
CORIOLIS = 0.2
precise = lax.Precision.HIGHEST


def padded(cells, sides, width):
    for axis, dim in sides:
        count = lax.axis_size(axis)
        ends = count - 1
        head = lax.slice_in_dim(cells, 0, width, axis=dim)
        tail = lax.slice_in_dim(cells, cells.shape[dim] - width, cells.shape[dim], axis=dim)
        cells = jnp.concatenate(
            [
                lax.ppermute(tail, axis, [(i, (i + 1) % count) for i in range(ends)]),
                cells,
                lax.ppermute(head, axis, [((i + 1) % count, i) for i in range(ends)]),
            ],
            axis=dim,
        )
    return cells


def thin_step(dynamic_vector, static_local, inner_cor):
    height = dynamic_vector[:, 0]
    bordered_array = padded(height, (("blk", 1), ("sub", 2)), 1)
    inner_depth = static_local[0]
    interior_indicator = static_local[1]
    grad_first = bordered_array[:, 2:, 1:-1] - bordered_array[:, :-2, 1:-1]
    grad_second = bordered_array[:, 1:-1, 2:] - bordered_array[:, 1:-1, :-2]
    first_new = interior_indicator * (
        (1.0 - FRICTION) * dynamic_vector[:, 1]
        + inner_cor * dynamic_vector[:, 2]
        - PRESSURE * grad_first
    )
    second_new = interior_indicator * (
        (1.0 - FRICTION) * dynamic_vector[:, 2]
        - inner_cor * dynamic_vector[:, 1]
        - PRESSURE * grad_second
    )
    fluxes = jnp.stack([inner_depth * first_new, inner_depth * second_new], axis=1)
    flux_wide = padded(fluxes, (("blk", 2), ("sub", 3)), 1)
    divergence = (
        flux_wide[:, 0, 2:, 1:-1]
        - flux_wide[:, 0, :-2, 1:-1]
        + (flux_wide[:, 1, 1:-1, 2:] - flux_wide[:, 1, 1:-1, :-2])
    )
    height_new = height - DIVERGE * divergence
    return jnp.stack([height_new, first_new, second_new], axis=1)


def observe(surface_height, obs_cell, obs_count, obs_value, obs_error):
    members = surface_height.shape[0]
    flat = surface_height.reshape(members, -1)
    cells = obs_cell.reshape(-1)
    picked = jnp.take(flat, cells, axis=1)
    pbar = jnp.mean(picked, axis=0)
    valid = jnp.arange(cells.shape[0], dtype=jnp.int32) < obs_count.reshape(())
    scale = jnp.where(valid, 1.0 / (obs_error.reshape(-1) * math.sqrt(members - 1)), 0.0)
    anomobs = (picked - pbar) * scale
    innov = (obs_value.reshape(-1) - pbar) * scale
    gram = jnp.dot(anomobs, anomobs.T, precision=precise)
    proj = jnp.dot(anomobs, innov, precision=precise)
    return jnp.concatenate([gram, proj[None]], axis=0)


def domain_reduction(packed):
    packed = lax.psum(packed, ("blk", "sub"))
    return packed


def transform(packed):
    members = packed.shape[1]
    eye = jnp.eye(members, dtype=jnp.float32)
    system = eye + packed[:members]
    proj = packed[members]
    factor_low = jnp.linalg.cholesky(system)
    mean_w = jax.scipy.linalg.cho_solve((factor_low, True), proj)
    scale = jnp.sqrt(jnp.sum(system * system))
    ystate = system / scale
    zstate = eye
    for sweep in range(NS_STEPS):
        factor = 1.5 * eye - 0.5 * jnp.dot(zstate, ystate, precision=precise)
        ystate = jnp.dot(ystate, factor, precision=precise)
        zstate = jnp.dot(factor, zstate, precision=precise)
    return mean_w[:, None] + zstate / jnp.sqrt(scale)


def shards(ensemble, basin_thickness, wet_indicator, obs_cell, obs_count, obs_value, obs_error):
    rows_dev = ensemble.shape[2]
    constant_fields = jnp.stack([basin_thickness, wet_indicator.astype(jnp.float32)])
    total_rows = rows_dev * lax.axis_size("blk")
    rows = (
        lax.axis_index("blk") * rows_dev + jnp.arange(-2, rows_dev + 2, dtype=jnp.int32)
    ).astype(jnp.float32)
    latitude_coupling = (CORIOLIS * (2.0 * (rows + 0.5) / total_rows - 1.0))[:, None]
    dynamic_vector = ensemble
    inner_cor = latitude_coupling[2:-2]
    for number in range(STEPS):
        dynamic_vector = thin_step(dynamic_vector, constant_fields, inner_cor)
    blocks = lax.all_to_all(dynamic_vector, "grid", split_axis=2, concat_axis=0, tiled=True)
    packed = domain_reduction(observe(blocks[:, 0], obs_cell, obs_count, obs_value, obs_error))
    weights = transform(packed)
    members = blocks.shape[0]
    flat = blocks.reshape(members, -1)
    center = jnp.mean(flat, axis=0)
    member_deviations = flat - center
    updated = center + jnp.dot(weights.T, member_deviations, precision=precise)
    return updated.reshape(members, 3, 1, blocks.shape[2], blocks.shape[3])


def solution(mesh):
    placed = (
        P(("copy", "grid"), None, "blk", "sub"),
        P(("copy", "blk"), "sub"),
        P(("copy", "blk"), "sub"),
        P(("copy", "blk"), "grid", "sub", None),
        P(("copy", "blk"), "grid", "sub"),
        P(("copy", "blk"), "grid", "sub", None),
        P(("copy", "blk"), "grid", "sub", None),
    )
    return jax.shard_map(
        shards,
        mesh=mesh,
        in_specs=placed,
        out_specs=P("copy", None, "blk", "grid", "sub"),
        check_vma=False,
    )
```

profile of v0, /device:TPU:0, one launch (start us, length us, event | category | flops | bytes accessed | tf_op | source)
XLA Modules:
  0.0 581.9 jit_solution(4712304430399835638)
XLA Ops:
  0.0 10.2 %fusion.67 = (f32[16,1,128,512]{3,2,1,0:T(8,128)}, f32[16,1,128,512]{3,2,1,0:T(8,128)}, f32[16,1,128,512]{3,2,1,0:T(8,128)S(1)}) fusion(f32[16,3,128,512]{3,2,1,0:T(8,128)} %param.7), kind=kLoop, calls=%fused_computation.164 | loop fusion | bytes 25165824 | tf_op jit(solution)/shard_map/slice | solution.py:45
  10.2 2.4 copy.107
  12.7 2.0 copy-done.5
  15.9 4.9 collective-permute-start.1
  20.9 1.5 collective-permute-done.1
  22.4 1.9 pad_maximum_fusion.54
  25.0 1.3 collective-permute-start.2
  26.9 3.2 collective-permute-start.3
  31.9 21.8 %multiply_bitcast_fusion.3 = (f32[16,1,128,512]{3,0,2,1:T(8,128)S(1)}, f32[16,128,512]{2,0,1:T(8,128)}, f32[16,1,128,512]{3,0,2,1:T(8,128)}, f32[16,128,512]{2,0,1:T(8,128)}) fusion(f32[128,512]{1,0:T(8,128)S(1)} %copy-done.8, f32[16,128,512]{2,0,1:T(8,128)} %bitcast.143, f32[16,1,512]{2,0,1:T(8,128)S(1)} %collective-permute-done.1, ...), kind=kLoop, calls=%fused_computation.76 | loop fusion | flops 25165824 | bytes 29967104 | tf_op jit(solution)/shard_map/stack | solution.py:53
  54.7 1.6 collective-permute-start.4
  56.3 4.7 collective-permute-start.5
  61.3 1.6 collective-permute-done.5
  62.8 2.1 pad_maximum_fusion.48
  65.0 2.8 copy.55
  67.8 1.3 collective-permute-start.6
  69.1 1.9 copy.57
  71.0 3.8 collective-permute-start.7
  74.8 2.2 copy.56
  77.0 2.6 copy.58
  79.7 11.1 %bitcast_subtract_fusion = (f32[16,128,512]{2,0,1:T(8,128)S(1)}, f32[16,1,128,512]{3,0,2,1:T(8,128)}) fusion(f32[16,1,128,512]{3,2,1,0:T(8,128)} %copy-done.4, f32[16,2,1,512]{3,0,2,1:T(8,128)S(1)} %collective-permute-done.4, f32[16,1,128,512]{3,0,2,1:T(8,128)} %get-tuple-element.17, f32[16,1,128,512]{3,0,2,1:T(8,128)} %copy-done.2, ...), kind=kLoop, calls=%fused_computation.72 | loop fusion | flops 17825792 | bytes 21135872 | tf_op jit(solution)/shard_map/sub | solution.py:60
  92.1 4.5 collective-permute-start.9
  96.7 1.6 collective-permute-done.9
  101.3 3.0 collective-permute-start.11
  105.9 17.2 %multiply_bitcast_fusion.1 = (f32[16,1,128,512]{3,0,2,1:T(8,128)S(1)}, f32[16,128,512]{2,0,1:T(8,128)}, f32[16,1,128,512]{3,0,2,1:T(8,128)S(1)}, f32[16,128,512]{2,0,1:T(8,128)}) fusion(f32[128,512]{1,0:T(8,128)} %param.8, f32[16,128,512]{2,0,1:T(8,128)} %copy-done.6, f32[16,1,512]{2,0,1:T(8,128)S(1)} %collective-permute-done.9, ...), kind=kLoop, calls=%fused_computation.74 | loop fusion | flops 25165824 | bytes 29967104 | tf_op jit(solution)/shard_map/stack | solution.py:53
  124.4 4.5 collective-permute-start.13
  129.4 1.5 collective-permute-done.13
  130.9 2.2 pad_maximum_fusion.44
  133.1 2.8 copy.63
  135.9 1.7 collective-permute-start.14
  138.9 3.0 collective-permute-start.15
  142.0 1.5 copy.64
  143.4 2.7 copy.66
  146.1 13.0 %fusion.5 = f32[16,1,128,512]{3,0,2,1:T(8,128)} fusion(f32[16,2,130,1]{3,0,2,1:T(8,128)} %copy.66, f32[16,2,1,512]{3,0,2,1:T(8,128)S(1)} %collective-permute-done.12, f32[16,2,1,512]{3,0,2,1:T(8,128)S(1)} %collective-permute-done.13, f32[16,1,128,512]{3,0,2,1:T(8,128)} %copy-done.1, f32[16,1,128,512]{3,0,2,1:T(8,128)} %copy-done, ...), kind=kLoop, calls=%fused_computation.9 | loop fusion | flops 18874368 | bytes 21135872 | tf_op jit(solution)/shard_map/sub | solution.py:60
  159.1 9.0 %pad_maximum_fusion = f32[16,3,128,512]{3,0,2,1:T(8,128)} fusion(f32[16,1,128,512]{3,0,2,1:T(8,128)} %bitcast.145, f32[16,1,128,512]{3,0,2,1:T(8,128)S(1)} %bitcast.144, f32[16,1,128,512]{3,0,2,1:T(8,128)} %fusion.5), kind=kLoop, calls=%fused_computation.2 | loop fusion | flops 6291456 | bytes 25165824 | tf_op jit(solution)/shard_map/stack | solution.py:61
  168.1 12.1 %copy.67 = f32[16,3,128,512]{3,0,1,2:T(8,128)} copy(f32[16,3,128,512]{3,0,2,1:T(8,128)} %pad_maximum_fusion) | data formatting | bytes 25165824 | tf_op jit(solution)/shard_map/stack | solution.py:61
  180.2 6.6 %all-to-all-start = ((f32[16,3,128,512]{3,0,1,2:T(8,128)}), f32[16,3,128,512]{3,0,1,2:T(8,128)}, u32[]{:S(2)}, u32[]{:S(2)}) async-start(f32[16,3,128,512]{3,0,1,2:T(8,128)} %copy.67), calls=%async_computation | async-start | bytes 25165824 | tf_op jit(solution)/shard_map/all_to_all | solution.py:113
  187.6 273.5 %all-to-all-done = f32[16,3,128,512]{3,0,1,2:T(8,128)} async-done(((f32[16,3,128,512]{3,0,1,2:T(8,128)}), f32[16,3,128,512]{3,0,1,2:T(8,128)}, u32[]{:S(2)}, u32[]{:S(2)}) %all-to-all-start) | async-done | bytes 12582944 | tf_op jit(solution)/shard_map/all_to_all | solution.py:113
  461.1 16.6 %copy.108 = f32[16,3,4,32,512]{4,3,1,0,2:T(8,128)} copy(f32[16,3,4,32,512]{4,0,1,3,2:T(8,128)} %bitcast.10) | data formatting | bytes 25165824 | tf_op jit(solution)/shard_map/all_to_all | solution.py:113
  477.8 5.0 slice.199
  482.8 6.9 %copy.79 = f32[64,1,32,512]{0,3,2,1:T(8,128)} copy(f32[64,1,32,512]{3,2,1,0:T(8,128)} %slice.199) | data formatting | bytes 8388608
  489.7 4.0 gather_fusion
  494.6 11.5 %psum.7 = f32[65,64]{0,1:T(8,128)S(1)} all-reduce(f32[65,64]{0,1:T(8,128)S(1)} %pad_maximum_fusion.59), channel_id=1, replica_groups=mesh['copy'=2,'grid'=4,'blk'=2,'sub'=2] {'blk','sub'}, use_global_device_ids=true, to_apply=%region_2.3 | all-reduce | flops 4160 | bytes 33280 | tf_op jit(solution)/shard_map/psum | solution.py:80
  511.4 11.1 %bitcast_reduce_fusion = f32[3,32,512]{2,1,0:T(8,128)S(1)} fusion(f32[16,3,4,32,512]{4,0,1,3,2:T(8,128)} %bitcast.10), kind=kLoop, calls=%fused_computation.160 | loop fusion | flops 3096576 | bytes 12779520 | tf_op jit(solution)/shard_map/reduce_sum | solution.py:118
  522.6 5.8 %cholesky.26 = f32[64,64]{1,0:T(8,128)S(1)} custom-call(f32[64,64]{1,0:T(8,128)S(1)} %fusion.39), custom_call_target="Cholesky" | custom-call | tf_op jit(solution)/shard_map/jit(cholesky)/cholesky | solution.py:89
  529.9 4.9 custom-call.10
  535.1 12.0 %reshape.118 = f32[64,49152]{1,0:T(8,128)} reshape(f32[4,16,3,32,512]{4,3,2,1,0:T(8,128)} %bitcast.139) | data formatting | bytes 25165824 | tf_op jit(solution)/shard_map/reshape | solution.py:117
  547.6 17.4 %convolution_add_fusion = f32[64,49152]{1,0:T(8,128)} fusion(f32[64,64]{1,0:T(8,128)S(1)} %fusion.28, f32[64,49152]{1,0:T(8,128)} %reshape.118, f32[49152]{0:T(1024)S(1)} %bitcast.147), kind=kOutput, calls=%fused_computation.1 | convolution fusion | flops 2422210560 | bytes 25378816 | tf_op jit(solution)/shard_map/dot_general | solution.py:120
  565.0 16.4 %copy.85 = f32[8,8,96,512]{3,2,1,0:T(8,128)} copy(f32[8,8,96,512]{3,1,2,0:T(8,128)} %bitcast.140) | data formatting | bytes 25165824
  (103 shorter events, 22.1 us)
Async XLA Ops:
  10.2 2.4 copy-start.4
  12.6 2.0 copy-start.5
  14.7 6.2 %collective-permute-start = (f32[16,1,512]{2,0,1:T(8,128)S(1)}, f32[16,1,512]{2,0,1:T(8,128)S(1)}, u32[]{:S(2)}, u32[]{:S(2)}) collective-permute-start(f32[16,1,512]{2,0,1:T(8,128)S(1)} %get-tuple-element.39), channel_id=1, source_target_pairs={{2,0},{3,1},{6,4},{7,5},{10,8},{11,9},{14,12},{15,13},{18,16},{19,... | collective-permute-start | bytes 98312 | tf_op jit(solution)/shard_map/ppermute | solution.py:29
  15.9 6.5 %collective-permute-start.1 = (f32[16,1,512]{2,0,1:T(8,128)S(1)}, f32[16,1,512]{2,0,1:T(8,128)S(1)}, u32[]{:S(2)}, u32[]{:S(2)}) collective-permute-start(f32[16,1,512]{2,0,1:T(8,128)S(1)} %get-tuple-element.38), channel_id=1, source_target_pairs={{0,2},{1,3},{4,6},{5,7},{8,10},{9,11},{12,14},{13,15},{16,18},{17,... | collective-permute-start | bytes 98312 | tf_op jit(solution)/shard_map/ppermute | solution.py:27
  20.8 9.3 %copy-start.9 = (s32[128,512]{1,0:T(8,128)S(1)}, s32[128,512]{1,0:T(8,128)}, u32[]{:S(2)}) copy-start(s32[128,512]{1,0:T(8,128)} %param.9) | copy-start | bytes 786436
  20.8 11.0 %copy-start.8 = (f32[128,512]{1,0:T(8,128)S(1)}, f32[128,512]{1,0:T(8,128)}, u32[]{:S(2)}) copy-start(f32[128,512]{1,0:T(8,128)} %param.8) | copy-start | bytes 786436
  25.0 5.3 collective-permute-start.2
  26.9 4.1 collective-permute-start.3
  53.7 9.2 %copy-start.2 = (f32[16,1,128,512]{3,0,2,1:T(8,128)}, f32[16,1,128,512]{3,0,2,1:T(8,128)S(1)}, u32[]{:S(2)}) copy-start(f32[16,1,128,512]{3,0,2,1:T(8,128)S(1)} %get-tuple-element.11) | copy-start | bytes 12582916
  53.7 9.2 %copy-start.3 = (f32[16,1,128,512]{3,0,2,1:T(8,128)S(1)}, f32[16,1,128,512]{3,0,2,1:T(8,128)}, u32[]{:S(2)}) copy-start(f32[16,1,128,512]{3,0,2,1:T(8,128)} %get-tuple-element.17) | copy-start | bytes 12582916
  54.7 6.6 %collective-permute-start.4 = (f32[16,2,1,512]{3,0,2,1:T(8,128)S(1)}, f32[16,2,1,512]{3,0,2,1:T(8,128)S(1)}, u32[]{:S(2)}, u32[]{:S(2)}) collective-permute-start(f32[16,2,1,512]{3,0,2,1:T(8,128)S(1)} %get-tuple-element.31), channel_id=1, source_target_pairs={{2,0},{3,1},{6,4},{7,5},{10,8},{11,9},{14,12},{15,13},{18,16},{19,... | collective-permute-start | bytes 196616 | tf_op jit(solution)/shard_map/ppermute | solution.py:29
  56.3 6.6 %collective-permute-start.5 = (f32[16,2,1,512]{3,0,2,1:T(8,128)S(1)}, f32[16,2,1,512]{3,0,2,1:T(8,128)S(1)}, u32[]{:S(2)}, u32[]{:S(2)}) collective-permute-start(f32[16,2,1,512]{3,0,2,1:T(8,128)S(1)} %get-tuple-element.30), channel_id=1, source_target_pairs={{0,2},{1,3},{4,6},{5,7},{8,10},{9,11},{12,14},{13,15},{16,18},{17,... | collective-permute-start | bytes 196616 | tf_op jit(solution)/shard_map/ppermute | solution.py:27
  67.8 7.0 %collective-permute-start.6 = (f32[16,2,130,1]{2,0,3,1:T(8,128)S(1)}, f32[16,2,130,1]{2,0,3,1:T(8,128)}, u32[]{:S(2)}, u32[]{:S(2)}) collective-permute-start(f32[16,2,130,1]{2,0,3,1:T(8,128)S(1)} %copy.55), channel_id=1, source_target_pairs={{1,0},{3,2},{5,4},{7,6},{9,8},{11,10},{13,12},{15,14},{17,16},{19,... | collective-permute-start | bytes 49928 | tf_op jit(solution)/shard_map/ppermute | solution.py:29
  71.0 6.0 %collective-permute-start.7 = (f32[16,2,130,1]{2,0,3,1:T(8,128)}, f32[16,2,130,1]{2,0,3,1:T(8,128)S(1)}, u32[]{:S(2)}, u32[]{:S(2)}) collective-permute-start(f32[16,2,130,1]{2,0,3,1:T(8,128)} %copy.57), channel_id=1, source_target_pairs={{0,1},{2,3},{4,5},{6,7},{8,9},{10,11},{12,13},{14,15},{16,17},{18,... | collective-permute-start | bytes 49928 | tf_op jit(solution)/shard_map/ppermute | solution.py:27
  90.8 7.5 %copy-start.6 = (f32[16,128,512]{2,0,1:T(8,128)}, f32[16,128,512]{2,0,1:T(8,128)S(1)}, u32[]{:S(2)}) copy-start(f32[16,128,512]{2,0,1:T(8,128)S(1)} %get-tuple-element.9) | copy-start | bytes 12582916
  90.8 5.9 %collective-permute-start.8 = (f32[16,1,512]{2,0,1:T(8,128)S(1)}, f32[16,1,512]{2,0,1:T(8,128)S(1)}, u32[]{:S(2)}, u32[]{:S(2)}) collective-permute-start(f32[16,1,512]{2,0,1:T(8,128)S(1)} %get-tuple-element.37), channel_id=1, source_target_pairs={{2,0},{3,1},{6,4},{7,5},{10,8},{11,9},{14,12},{15,13},{18,16},{19,... | collective-permute-start | bytes 98312 | tf_op jit(solution)/shard_map/ppermute | solution.py:29
  92.1 6.1 %collective-permute-start.9 = (f32[16,1,512]{2,0,1:T(8,128)S(1)}, f32[16,1,512]{2,0,1:T(8,128)S(1)}, u32[]{:S(2)}, u32[]{:S(2)}) collective-permute-start(f32[16,1,512]{2,0,1:T(8,128)S(1)} %get-tuple-element.36), channel_id=1, source_target_pairs={{0,2},{1,3},{4,6},{5,7},{8,10},{9,11},{12,14},{13,15},{16,18},{17,... | collective-permute-start | bytes 98312 | tf_op jit(solution)/shard_map/ppermute | solution.py:27
  99.3 5.0 collective-permute-start.10
  101.3 3.9 collective-permute-start.11
  123.1 7.8 %copy-start = (f32[16,1,128,512]{3,0,2,1:T(8,128)}, f32[16,1,128,512]{3,0,2,1:T(8,128)S(1)}, u32[]{:S(2)}) copy-start(f32[16,1,128,512]{3,0,2,1:T(8,128)S(1)} %get-tuple-element.5) | copy-start | bytes 12582916
  123.1 7.8 %copy-start.1 = (f32[16,1,128,512]{3,0,2,1:T(8,128)}, f32[16,1,128,512]{3,0,2,1:T(8,128)S(1)}, u32[]{:S(2)}) copy-start(f32[16,1,128,512]{3,0,2,1:T(8,128)S(1)} %get-tuple-element.15) | copy-start | bytes 12582916
  123.1 6.2 %collective-permute-start.12 = (f32[16,2,1,512]{3,0,2,1:T(8,128)S(1)}, f32[16,2,1,512]{3,0,2,1:T(8,128)S(1)}, u32[]{:S(2)}, u32[]{:S(2)}) collective-permute-start(f32[16,2,1,512]{3,0,2,1:T(8,128)S(1)} %get-tuple-element.29), channel_id=1, source_target_pairs={{2,0},{3,1},{6,4},{7,5},{10,8},{11,9},{14,12},{15,13},{18,16},{19,... | collective-permute-start | bytes 196616 | tf_op jit(solution)/shard_map/ppermute | solution.py:29
  124.4 6.4 %collective-permute-start.13 = (f32[16,2,1,512]{3,0,2,1:T(8,128)S(1)}, f32[16,2,1,512]{3,0,2,1:T(8,128)S(1)}, u32[]{:S(2)}, u32[]{:S(2)}) collective-permute-start(f32[16,2,1,512]{3,0,2,1:T(8,128)S(1)} %get-tuple-element.28), channel_id=1, source_target_pairs={{0,2},{1,3},{4,6},{5,7},{8,10},{9,11},{12,14},{13,15},{16,18},{17,... | collective-permute-start | bytes 196616 | tf_op jit(solution)/shard_map/ppermute | solution.py:27
  135.9 6.0 %collective-permute-start.14 = (f32[16,2,130,1]{2,0,3,1:T(8,128)S(1)}, f32[16,2,130,1]{2,0,3,1:T(8,128)S(1)}, u32[]{:S(2)}, u32[]{:S(2)}) collective-permute-start(f32[16,2,130,1]{2,0,3,1:T(8,128)S(1)} %copy.63), channel_id=1, source_target_pairs={{1,0},{3,2},{5,4},{7,6},{9,8},{11,10},{13,12},{15,14},{17,16},{19,... | collective-permute-start | bytes 49928 | tf_op jit(solution)/shard_map/ppermute | solution.py:29
  138.9 4.5 collective-permute-start.15
  146.1 13.0 %copy-start.7 = (f32[16,128,512]{2,0,1:T(8,128)S(1)}, f32[16,128,512]{2,0,1:T(8,128)}, u32[]{:S(2)}) copy-start(f32[16,128,512]{2,0,1:T(8,128)} %get-tuple-element.6) | copy-start | bytes 12582916
  180.2 7.4 %copy-start.11 = (s32[1,1,1,64]{3,2,1,0:T(1,128)S(1)}, s32[1,1,1,64]{3,2,1,0:T(1,128)}, u32[]{:S(2)}) copy-start(s32[1,1,1,64]{3,2,1,0:T(1,128)} %param.10) | copy-start | bytes 772
  180.2 280.9 %all-to-all-start = ((f32[16,3,128,512]{3,0,1,2:T(8,128)}), f32[16,3,128,512]{3,0,1,2:T(8,128)}, u32[]{:S(2)}, u32[]{:S(2)}) async-start(f32[16,3,128,512]{3,0,1,2:T(8,128)} %copy.67), calls=%async_computation | async-start | bytes 25165824 | tf_op jit(solution)/shard_map/all_to_all | solution.py:113
  482.8 11.1 %copy-start.10 = (f32[1,1,1,64]{3,2,1,0:T(1,128)S(1)}, f32[1,1,1,64]{3,2,1,0:T(1,128)}, u32[]{:S(2)}) copy-start(f32[1,1,1,64]{3,2,1,0:T(1,128)} %param.13) | copy-start | bytes 772
  482.8 11.5 %copy-start.12 = (f32[1,1,1,64]{3,2,1,0:T(1,128)S(1)}, f32[1,1,1,64]{3,2,1,0:T(1,128)}, u32[]{:S(2)}) copy-start(f32[1,1,1,64]{3,2,1,0:T(1,128)} %param.12) | copy-start | bytes 772
where the time goes:
time: 588 us; the launch traced here: 582 us
  waiting for transfers between devices  280 us (48%)
  local copies, waits for them, and re-layouts  112 us (19%)
  other arithmetic  104 us (18%)
  starting transfers between devices  49.3 us (8%)
  matrix products  22.2 us (4%)
  blocking collectives  11.5 us (2%)
    all_to_all x1, waiting for transfers between devices, shards(): lax.all_to_all(dynamic_vector, 'grid', split_axis=2, concat_axis=0, tiled...  273 us
    another operation x4, other arithmetic, thin_step(): jnp.stack([inner_depth * first_new, inner_depth * second_new], axis=1)  40 us
    ppermute x8, starting transfers between devices, padded(): lax.ppermute(tail, axis, [(i, (i + 1) % count) for i in range(ends)])  31.7 us
    unnamed x30, local copies, waits for them, and re-layouts  27.9 us
    sub x2, other arithmetic, thin_step(): height_new = height - DIVERGE * divergence  24.1 us
    dot_general x1, matrix products, shards(): updated = center + jnp.dot(weights.T, member_deviations, precision=precise)  17.4 us
    all_to_all x1, local copies, waits for them, and re-layouts, shards(): lax.all_to_all(dynamic_vector, 'grid', split_axis=2, concat_axis=0, tiled...  16.6 us
    another operation x1, local copies, waits for them, and re-layouts, thin_step(): return jnp.stack([height_new, first_new, second_new], axis=1)  12.1 us
  transfers between devices with their start and end apart: 17, of which 7 were waited for; matrix products, arithmetic and copies ran while one was open for 2% of the time, Pallas kernels for 0%

commit v1 on v0

v1 whole, which is shorter than its diff:
```python
import math

import jax
import jax.numpy as jnp
from jax import lax
from jax.experimental import pallas as pl
from jax.experimental.pallas import tpu as pltpu
from jax.sharding import PartitionSpec as P

STEPS = 2
NS_STEPS = 8
HALO = 4
LANES = 128

FRICTION = 0.05
PRESSURE = 0.35
DIVERGE = 0.35
CORIOLIS = 0.2
precise = lax.Precision.HIGHEST


def neighbours(head, tail, axis):
    count = lax.axis_size(axis)
    if count == 2:
        index = lax.axis_index(axis)
        got = lax.ppermute(jnp.where(index == 0, tail, head), axis, [(0, 1), (1, 0)])
        zero = jnp.zeros_like(got)
        return jnp.where(index == 1, got, zero), jnp.where(index == 0, got, zero)
    before = lax.ppermute(tail, axis, [(i, i + 1) for i in range(count - 1)])
    after = lax.ppermute(head, axis, [(i + 1, i) for i in range(count - 1)])
    return before, after


def forecast_kernel(x_ref, rows_ref, cols_ref, depth_ref, wet_ref, inside_ref, cor_ref, h_ref, u_ref, v_ref):
    core_rows, core_cols = x_ref.shape[2], x_ref.shape[3]
    rows = core_rows + 2 * HALO
    cols = core_cols + LANES

    def full(field):
        tall = jnp.concatenate([x_ref[0, field], rows_ref[0, field]], axis=0)
        return jnp.concatenate([tall, cols_ref[0, field]], axis=1)

    def along_first(q):
        return pltpu.roll(q, rows - 1, 0) - pltpu.roll(q, 1, 0)

    def along_second(q):
        return pltpu.roll(q, cols - 1, 1) - pltpu.roll(q, 1, 1)

    h, u, v = full(0), full(1), full(2)
    wet = wet_ref[...]
    depth = depth_ref[...]
    inside = inside_ref[...]
    cor = jnp.broadcast_to(cor_ref[:, :1], (rows, cols))
    for number in range(STEPS):
        first = wet * ((1.0 - FRICTION) * u + cor * v - PRESSURE * along_first(h))
        second = wet * ((1.0 - FRICTION) * v - cor * u - PRESSURE * along_second(h))
        h = inside * (h - DIVERGE * (along_first(depth * first) + along_second(depth * second)))
        u, v = first, second
    for ref, value in ((h_ref, h), (u_ref, u), (v_ref, v)):
        ref[:, 0] = value[:core_rows, :core_cols].reshape(ref.shape[0], ref.shape[2], core_cols)


def forecast(ensemble, basin_thickness, wet_indicator):
    members, fields, core_rows, core_cols = ensemble.shape
    parts = lax.axis_size("grid")
    static = jnp.stack([basin_thickness, wet_indicator.astype(jnp.float32)])
    flat = ensemble.reshape(members * fields, core_rows, core_cols)

    def edge(lo, hi):
        return jnp.concatenate([flat[:, lo:hi], static[:, lo:hi]], axis=0)

    before, after = neighbours(edge(0, HALO), edge(core_rows - HALO, core_rows), "blk")
    row_halo = jnp.concatenate([after, before], axis=1)

    def side(lo, hi):
        core = jnp.concatenate([flat[:, :, lo:hi], static[:, :, lo:hi]], axis=0)
        return jnp.concatenate([core, row_halo[:, :, lo:hi]], axis=1)

    before, after = neighbours(side(0, HALO), side(core_cols - HALO, core_cols), "sub")
    gap = jnp.zeros(before.shape[:2] + (LANES - 2 * HALO,), jnp.float32)
    col_halo = jnp.concatenate([after, gap, before], axis=2)
    count = members * fields

    def whole(which):
        tall = jnp.concatenate([static[which], row_halo[count + which]], axis=0)
        return jnp.concatenate([tall, col_halo[count + which]], axis=1)

    depth, wet = whole(0), whole(1)
    rows, cols = depth.shape

    def offset(size, total):
        place = jnp.arange(total, dtype=jnp.int32)
        return jnp.where(place >= total - HALO, place - total, place)

    def within(axis, size, total):
        place = offset(size, total)
        index, ends = lax.axis_index(axis), lax.axis_size(axis) - 1
        middle = (place >= 0) & (place < size)
        past = (place >= size) & (place < size + HALO) & (index < ends)
        return middle | past | ((place < 0) & (index > 0))

    inside = (within("blk", core_rows, rows)[:, None] & within("sub", core_cols, cols)[None, :]).astype(jnp.float32)
    total_rows = core_rows * lax.axis_size("blk")
    line = (lax.axis_index("blk") * core_rows + offset(core_rows, rows)).astype(jnp.float32)
    cor = CORIOLIS * (2.0 * (line + 0.5) / total_rows - 1.0)
    cor = jnp.broadcast_to(cor[:, None], (rows, LANES))
    lines = core_rows // parts

    def fixed(shape):
        return pl.BlockSpec(shape, lambda m: (0,) * len(shape))

    shape = jax.ShapeDtypeStruct((parts, members, lines, core_cols), jnp.float32)
    spec = pl.BlockSpec((parts, 1, lines, core_cols), lambda m: (0, m, 0, 0))
    return pl.pallas_call(
        forecast_kernel,
        grid=(members,),
        in_specs=[
            pl.BlockSpec((1, fields, core_rows, core_cols), lambda m: (m, 0, 0, 0)),
            pl.BlockSpec((1, fields, 2 * HALO, core_cols), lambda m: (m, 0, 0, 0)),
            pl.BlockSpec((1, fields, rows, LANES), lambda m: (m, 0, 0, 0)),
            fixed((rows, cols)),
            fixed((rows, cols)),
            fixed((rows, cols)),
            fixed((rows, LANES)),
        ],
        out_specs=[spec] * 3,
        out_shape=[shape] * 3,
        compiler_params=pltpu.CompilerParams(dimension_semantics=("arbitrary",)),
        name="forecast",
    )(
        ensemble,
        row_halo[:count].reshape(members, fields, 2 * HALO, core_cols),
        col_halo[:count].reshape(members, fields, rows, LANES),
        depth,
        wet,
        inside,
        cor,
    )


def observe(surface_height, obs_cell, obs_count, obs_value, obs_error):
    members = surface_height.shape[0]
    flat = surface_height.reshape(members, -1)
    cells = obs_cell.reshape(-1)
    picked = jnp.take(flat, cells, axis=1)
    pbar = jnp.mean(picked, axis=0)
    valid = jnp.arange(cells.shape[0], dtype=jnp.int32) < obs_count.reshape(())
    scale = jnp.where(valid, 1.0 / (obs_error.reshape(-1) * math.sqrt(members - 1)), 0.0)
    anomobs = (picked - pbar) * scale
    innov = (obs_value.reshape(-1) - pbar) * scale
    gram = jnp.dot(anomobs, anomobs.T, precision=precise)
    proj = jnp.dot(anomobs, innov, precision=precise)
    return jnp.concatenate([gram, proj[None]], axis=0)


def domain_reduction(packed):
    for axis in ("sub", "blk"):
        if lax.axis_size(axis) == 2:
            packed = packed + lax.ppermute(packed, axis, [(0, 1), (1, 0)])
        else:
            packed = lax.psum(packed, axis)
    return packed


def transform(packed):
    members = packed.shape[1]
    eye = jnp.eye(members, dtype=jnp.float32)
    system = eye + packed[:members]
    proj = packed[members]
    factor_low = jnp.linalg.cholesky(system)
    mean_w = jax.scipy.linalg.cho_solve((factor_low, True), proj)
    scale = jnp.sqrt(jnp.sum(system * system))
    ystate = system / scale
    zstate = eye
    for sweep in range(NS_STEPS):
        factor = 1.5 * eye - 0.5 * jnp.dot(zstate, ystate, precision=precise)
        ystate = jnp.dot(ystate, factor, precision=precise)
        zstate = jnp.dot(factor, zstate, precision=precise)
    return mean_w[:, None] + zstate / jnp.sqrt(scale)


def shards(ensemble, basin_thickness, wet_indicator, obs_cell, obs_count, obs_value, obs_error):
    pieces = forecast(ensemble, basin_thickness, wet_indicator)
    blocks = []
    for piece in pieces:
        got = lax.all_to_all(piece, "grid", split_axis=0, concat_axis=0, tiled=True)
        blocks.append(got.reshape((-1,) + got.shape[2:]))
    packed = domain_reduction(observe(blocks[0], obs_cell, obs_count, obs_value, obs_error))
    weights = transform(packed)
    members = weights.shape[0]
    mixing = weights - jnp.mean(weights, axis=0) + 1.0 / members
    updated = [
        lax.dot_general(mixing, block, (((0,), (0,)), ((), ())), precision=lax.Precision.HIGH)
        for block in blocks
    ]
    return jnp.stack(updated, axis=1)[:, :, None]


def solution(mesh):
    placed = (
        P(("copy", "grid"), None, "blk", "sub"),
        P(("copy", "blk"), "sub"),
        P(("copy", "blk"), "sub"),
        P(("copy", "blk"), "grid", "sub", None),
        P(("copy", "blk"), "grid", "sub"),
        P(("copy", "blk"), "grid", "sub", None),
        P(("copy", "blk"), "grid", "sub", None),
    )
    return jax.shard_map(
        shards,
        mesh=mesh,
        in_specs=placed,
        out_specs=P("copy", None, "blk", "grid", "sub"),
        check_vma=False,
    )
```

time: 588 us -> 400 us (0.68)
  waiting for transfers between devices: 280 us -> 135 us
  blocking collectives: 11.5 us -> 99.6 us
  other arithmetic: 104 us -> 36.4 us
  local copies, waits for them, and re-layouts: 112 us -> 51 us
  starting transfers between devices: 49.3 us -> 14.9 us
  Pallas kernels: 0 us -> 23.6 us
  matrix products: 22.2 us -> 30.3 us
    all_to_all x1 -> x2, waiting for transfers between devices: 273 us -> 126 us  [shards(): got = lax.all_to_all(piece, 'grid', split_axis=0, concat_axis=0, tiled=True)]
    all_to_all x0 -> x1, blocking collectives: none -> 99.6 us  [shards(): got = lax.all_to_all(piece, 'grid', split_axis=0, concat_axis=0, tiled=True)]
    another operation x5 -> x0, other arithmetic: 49.1 us -> none  [the longest x4 40 us: thin_step(): jnp.stack([inner_depth * first_new, inner_depth * second_new], axis=1)]
    ppermute x16 -> x4, starting transfers between devices: 42.7 us -> 4.59 us  [the longest x2 3.03 us: neighbours(): lax.ppermute(jnp.where(index == 0, tail, head), axis, [(0, 1), (1, 0)])]
    sub x2 -> x0, other arithmetic: 24.1 us -> none  [thin_step(): height_new = height - DIVERGE * divergence]
    pallas_call x0 -> x1, Pallas kernels: none -> 23.6 us  [forecast(): pl.pallas_call(forecast_kernel, grid=(members,), in_specs=[pl.BlockSpec((...]
    unnamed x30 -> x23, local copies, waits for them, and re-layouts: 27.9 us -> 6.62 us
    slice x13 -> x3, local copies, waits for them, and re-layouts: 26.8 us -> 7.53 us  [the longest x1 4 us: side(): core = jnp.concatenate([flat[:, :, lo:hi], static[:, :, lo:hi]], axis=0)]
  transfers between devices with their start and end apart: 17 -> 6, of which waited for: 7 -> 6; matrix products, arithmetic and copies ran while one was open for 2% -> 15% of each run, Pallas kernels for 0% -> 0%
where the time goes in v1:
time: 400 us; the launch traced here: 393 us
  waiting for transfers between devices  135 us (34%)
  blocking collectives  99.6 us (25%)
  local copies, waits for them, and re-layouts  51 us (13%)
  other arithmetic  36.4 us (9%)
  matrix products  30.3 us (8%)
  Pallas kernels  23.6 us (6%)
  starting transfers between devices  14.9 us (4%)
    all_to_all x2, waiting for transfers between devices, shards(): got = lax.all_to_all(piece, 'grid', split_axis=0, concat_axis=0, tiled=True)  126 us
    all_to_all x1, blocking collectives, shards(): got = lax.all_to_all(piece, 'grid', split_axis=0, concat_axis=0, tiled=True)  99.6 us
    dot_general x3, matrix products, shards(): lax.dot_general(mixing, block, (((0,), (0,)), ((), ())), precision=lax.Pr...  25.4 us
    pallas_call x1, Pallas kernels, forecast(): pl.pallas_call(forecast_kernel, grid=(members,), in_specs=[pl.BlockSpec((...  23.6 us
    broadcast_in_dim x1, local copies, waits for them, and re-layouts, shards(): return jnp.stack(updated, axis=1)[:, :, None]  16.6 us
    broadcast_in_dim x1, other arithmetic, shards(): return jnp.stack(updated, axis=1)[:, :, None]  10.4 us
    all_to_all x2, starting transfers between devices, shards(): got = lax.all_to_all(piece, 'grid', split_axis=0, concat_axis=0, tiled=True)  10.3 us
  transfers between devices with their start and end apart: 6, of which 6 were waited for; matrix products, arithmetic and copies ran while one was open for 15% of the time, Pallas kernels for 0%

profile of v1, /device:TPU:0, one launch (start us, length us, event | category | flops | bytes accessed | tf_op | source)
XLA Modules:
  0.0 393.2 jit_solution(8015415865701776200)
XLA Ops:
  0.0 1.6 fusion.88
  1.6 1.7 fusion.89
  3.3 0.9 fusion.31
  4.2 3.0 collective-permute-start
  7.4 0.8 and_convert_fusion.inside_ref
  8.2 4.0 %fusion.87 = (f32[48,128,4]{2,1,0:T(8,128)S(1)}, f32[48,128,4]{2,1,0:T(8,128)S(1)}) fusion(f32[48,128,512]{2,1,0:T(8,128)} %bitcast.126), kind=kLoop, calls=%fused_computation.142 | loop fusion | bytes 393216 | tf_op jit(solution)/shard_map/slice | solution.py:76
  12.2 4.5 %collective-permute-done = f32[50,4,512]{2,1,0:T(4,128)S(1)} collective-permute-done((f32[50,4,512]{2,1,0:T(4,128)S(1)}, f32[50,4,512]{2,1,0:T(4,128)S(1)}, u32[]{:S(2)}, u32[]{:S(2)}) %collective-permute-start) | collective-permute-done | bytes 409632 | tf_op jit(solution)/shard_map/ppermute | solution.py:26
  16.9 0.2 fusion.34
  17.1 1.1 fusion.29
  18.1 2.4 fusion.8
  20.6 2.8 copy.108
  23.4 0.8 fusion.49
  24.1 0.9 collective-permute-done.1
  25.0 0.8 broadcast_select_fusion.3
  25.9 2.1 copy.110
  27.9 3.3 copy.111
  31.2 2.9 pad_maximum_fusion.2
  34.2 2.0 slice.102
  36.2 1.0 pad_maximum_fusion.5
  37.1 0.7 broadcast_in_dim.49.cor_ref
  37.9 23.6 %forecast.1 = (f32[4,16,32,512]{3,2,1,0:T(8,128)}, f32[4,16,32,512]{3,2,1,0:T(8,128)}, f32[4,16,32,512]{3,2,1,0:T(8,128)}) custom-call(f32[16,3,128,512]{3,2,1,0:T(8,128)} %x_ref.1, f32[16,3,8,512]{3,2,1,0:T(8,128)} %bitcast.129, f32[16,3,136,128]{3,2,1,0:T(8,128)} %bitcast.128, f32[136,640]{1,0:T(8,128)} %get-tuple-element.31.depth_ref, ...), custom_call_target="tpu_custom_call" | custom-call | tf_op jit(solution)/shard_map/forecast/pallas_call | solution.py:114
  61.5 99.6 %all_to_all.15 = f32[4,16,32,512]{3,2,1,0:T(8,128)} all-to-all(f32[4,16,32,512]{3,2,1,0:T(8,128)} %get-tuple-element.8), channel_id=1, replica_groups=mesh['copy'=2,'grid'=4,'blk'=2,'sub'=2] {'grid'}, dimensions={0} | all-to-all | bytes 8388608 | tf_op jit(solution)/shard_map/all_to_all | solution.py:186
  161.1 5.2 %all-to-all-start.1 = ((f32[4,16,32,512]{3,2,1,0:T(8,128)}), f32[4,16,32,512]{3,2,1,0:T(8,128)}, u32[]{:S(2)}, u32[]{:S(2)}) async-start(f32[4,16,32,512]{3,2,1,0:T(8,128)} %get-tuple-element.9), calls=%async_computation.1 | async-start | bytes 8388608 | tf_op jit(solution)/shard_map/all_to_all | solution.py:186
  167.1 6.6 %copy.135 = f32[8,8,32,512]{3,1,2,0:T(8,128)} copy(f32[8,8,32,512]{3,2,1,0:T(8,128)} %bitcast.123) | data formatting | bytes 8388608
  173.7 6.9 %copy.112 = f32[64,16384]{0,1:T(8,128)} copy(f32[64,16384]{1,0:T(8,128)} %bitcast.127) | data formatting | bytes 8388608 | tf_op jit(solution)/shard_map/reshape;reshape | solution.py:143
  180.6 4.0 %gather_fusion = f32[64,64]{1,0:T(8,128)S(1)} fusion(f32[64,16384]{0,1:T(8,128)} %copy.112, s32[1024]{0:T(1024)S(1)} %pad_clamp_fusion), kind=kCustom, calls=%fused_computation | custom fusion | bytes 33024 | tf_op jit(solution)/shard_map/jit(_take)/gather | solution.py:145
  184.5 0.2 select_reduce_fusion.1
  184.7 0.3 fusion.46
  185.1 0.3 fusion.42
  185.5 1.2 collective-permute-done.2
  186.8 1.5 collective-permute-start.3
  188.4 2.3 collective-permute-done.3
  190.7 0.6 slice_add_fusion
  191.4 5.8 %cholesky.26 = f32[64,64]{1,0:T(8,128)S(1)} custom-call(f32[64,64]{1,0:T(8,128)S(1)} %fusion.41), custom_call_target="Cholesky" | custom-call | tf_op jit(solution)/shard_map/jit(cholesky)/cholesky | solution.py:170
  197.5 0.7 compare_reduce_fusion
  198.2 0.6 fusion.35
  198.8 4.9 %custom-call.10 = f32[1,64,64]{1,2,0:T(8,128)S(1)} custom-call(f32[1,64,64]{2,1,0:T(8,128)S(1)} %fusion.35), custom_call_target="InvertDiagBlocksLowerTriangular" | custom-call | tf_op jit(solution)/shard_map/jit(_cho_solve)/triangular_solve | solution.py:171
  204.6 54.7 %all-to-all-done.1 = f32[4,16,32,512]{3,2,1,0:T(8,128)} async-done(((f32[4,16,32,512]{3,2,1,0:T(8,128)}), f32[4,16,32,512]{3,2,1,0:T(8,128)}, u32[]{:S(2)}, u32[]{:S(2)}) %all-to-all-start.1) | async-done | bytes 4194336 | tf_op jit(solution)/shard_map/all_to_all | solution.py:186
  259.3 5.0 %all-to-all-start.2 = ((f32[4,16,32,512]{3,2,1,0:T(8,128)}), f32[4,16,32,512]{3,2,1,0:T(8,128)}, u32[]{:S(2)}, u32[]{:S(2)}) async-start(f32[4,16,32,512]{3,2,1,0:T(8,128)} %get-tuple-element.10), calls=%async_computation.2 | async-start | bytes 8388608 | tf_op jit(solution)/shard_map/all_to_all | solution.py:186
  264.7 0.2 fusion.20
  265.1 0.2 fusion.65
  268.6 0.2 fusion.90
  268.8 8.3 %fusion.11 = f32[64,1,32,512]{3,0,2,1:T(8,128)} fusion(f32[64,32,512]{2,1,0:T(8,128)} %bitcast.124, f32[64,64]{1,0:T(8,128)S(1)} %get-tuple-element.30, f32[64]{0:T(128)S(1)} %broadcast_multiply_fusion), kind=kOutput, calls=%fused_computation.16 | convolution fusion | flops 402661376 | bytes 8405248 | tf_op jit(solution)/shard_map/dot_general | solution.py:193
  277.1 8.3 %fusion.14 = f32[64,1,32,512]{3,0,2,1:T(8,128)} fusion(f32[64,32,512]{2,1,0:T(8,128)} %bitcast.28, f32[64,64]{1,0:T(8,128)S(1)} %get-tuple-element.30, f32[64]{0:T(128)S(1)} %broadcast_multiply_fusion), kind=kOutput, calls=%fused_computation.17 | convolution fusion | flops 402661376 | bytes 8405248 | tf_op jit(solution)/shard_map/dot_general | solution.py:193
  285.4 71.5 %all-to-all-done.2 = f32[4,16,32,512]{3,2,1,0:T(8,128)} async-done(((f32[4,16,32,512]{3,2,1,0:T(8,128)}), f32[4,16,32,512]{3,2,1,0:T(8,128)}, u32[]{:S(2)}, u32[]{:S(2)}) %all-to-all-start.2) | async-done | bytes 4194336 | tf_op jit(solution)/shard_map/all_to_all | solution.py:186
  357.0 8.8 %fusion.17 = f32[64,1,32,512]{3,0,2,1:T(8,128)} fusion(f32[64,32,512]{2,1,0:T(8,128)} %bitcast.31, f32[64,64]{1,0:T(8,128)S(1)} %get-tuple-element.30, f32[64]{0:T(128)S(1)} %broadcast_multiply_fusion), kind=kOutput, calls=%fused_computation.18 | convolution fusion | flops 402661376 | bytes 8405248 | tf_op jit(solution)/shard_map/dot_general | solution.py:193
  365.8 10.4 %maximum_bitcast_fusion = f32[64,3,1,32,512]{4,0,3,1,2:T(8,128)} fusion(f32[64,1,32,512]{3,0,2,1:T(8,128)} %fusion.17, f32[64,1,32,512]{3,0,2,1:T(8,128)} %fusion.14, f32[64,1,32,512]{3,0,2,1:T(8,128)S(1)} %copy-done), kind=kLoop, calls=%fused_computation.1 | loop fusion | flops 6291456 | bytes 25165824 | tf_op jit(solution)/shard_map/broadcast_in_dim | solution.py:196
  376.1 16.6 %copy.124 = f32[64,3,1,32,512]{4,3,2,1,0:T(8,128)} copy(f32[64,3,1,32,512]{4,0,3,1,2:T(8,128)} %maximum_bitcast_fusion) | data formatting | bytes 25165824 | tf_op jit(solution)/shard_map/broadcast_in_dim | solution.py:196
  (69 shorter events, 4.6 us)
Async XLA Ops:
  3.3 8.9 %copy-start.3 = (f32[1,128,512]{2,1,0:T(8,128)}, f32[1,128,512]{2,1,0:T(8,128)S(1)}, u32[]{:S(2)}) copy-start(f32[1,128,512]{2,1,0:T(8,128)S(1)} %get-tuple-element.24) | copy-start | bytes 786436
  4.2 12.5 %collective-permute-start = (f32[50,4,512]{2,1,0:T(4,128)S(1)}, f32[50,4,512]{2,1,0:T(4,128)S(1)}, u32[]{:S(2)}, u32[]{:S(2)}) collective-permute-start(f32[50,4,512]{2,1,0:T(4,128)S(1)} %fusion.31), channel_id=1, source_target_pairs={{0,2},{2,0},{1,3},{3,1},{4,6},{6,4},{5,7},{7,5},{8,10},{10,8},{9,1... | collective-permute-start | bytes 1228808 | tf_op jit(solution)/shard_map/ppermute | solution.py:26
  12.2 5.9 %copy-start.5 = (f32[128,512]{1,0:T(8,128)S(1)}, f32[128,512]{1,0:T(8,128)}, u32[]{:S(2)}) copy-start(f32[128,512]{1,0:T(8,128)} %param.8) | copy-start | bytes 786436
  16.7 1.4 copy-start.4
  16.9 1.3 copy-start.1
  16.9 1.3 copy-start.2
  23.4 1.7 collective-permute-start.1
  34.2 2.0 copy-start.6
  34.2 2.0 copy-start.7
  161.1 5.9 %copy-start.8 = (s32[1,1,1,64]{3,2,1,0:T(1,128)S(1)}, s32[1,1,1,64]{3,2,1,0:T(1,128)}, u32[]{:S(2)}) copy-start(s32[1,1,1,64]{3,2,1,0:T(1,128)} %param.10) | copy-start | bytes 772
  161.1 6.0 %copy-start.9 = (f32[1,1,1,64]{3,2,1,0:T(1,128)S(1)}, f32[1,1,1,64]{3,2,1,0:T(1,128)}, u32[]{:S(2)}) copy-start(f32[1,1,1,64]{3,2,1,0:T(1,128)} %param.13) | copy-start | bytes 772
  161.1 98.2 %all-to-all-start.1 = ((f32[4,16,32,512]{3,2,1,0:T(8,128)}), f32[4,16,32,512]{3,2,1,0:T(8,128)}, u32[]{:S(2)}, u32[]{:S(2)}) async-start(f32[4,16,32,512]{3,2,1,0:T(8,128)} %get-tuple-element.9), calls=%async_computation.1 | async-start | bytes 8388608 | tf_op jit(solution)/shard_map/all_to_all | solution.py:186
  173.7 11.4 %copy-start.10 = (f32[1,1,1,64]{3,2,1,0:T(1,128)S(1)}, f32[1,1,1,64]{3,2,1,0:T(1,128)}, u32[]{:S(2)}) copy-start(f32[1,1,1,64]{3,2,1,0:T(1,128)} %param.12) | copy-start | bytes 772
  185.5 1.2 collective-permute-start.2
  186.8 3.9 collective-permute-start.3
  259.3 97.6 %all-to-all-start.2 = ((f32[4,16,32,512]{3,2,1,0:T(8,128)}), f32[4,16,32,512]{3,2,1,0:T(8,128)}, u32[]{:S(2)}, u32[]{:S(2)}) async-start(f32[4,16,32,512]{3,2,1,0:T(8,128)} %get-tuple-element.10), calls=%async_computation.2 | async-start | bytes 8388608 | tf_op jit(solution)/shard_map/all_to_all | solution.py:186
  357.0 8.8 %copy-start = (f32[64,1,32,512]{3,0,2,1:T(8,128)S(1)}, f32[64,1,32,512]{3,0,2,1:T(8,128)}, u32[]{:S(2)}) copy-start(f32[64,1,32,512]{3,0,2,1:T(8,128)} %fusion.11) | copy-start | bytes 12582916
